TPU v7x, 128 devices: a whole 4x4x4 slice. The times are simulated.
128 devices in a mesh: dp: 4 (over y_lo, core), ctx: 32 (over z, x, y_hi).
Axes of the slice: x: 4, y: 4 (y_hi: 2, y_lo: 2; y = y_hi * 2 + y_lo), z: 4, core: 2. Of those that a mesh axis runs over, the one named last changes fastest.
Arguments:
- queries: bfloat16 [4, 32768, 1024], P('dp', 'ctx'), may hold values from -160 to 160
- keys: bfloat16 [4, 32768, 1024], P('dp', 'ctx'), may hold values from -14 to 14
- values: bfloat16 [4, 32768, 1024], P('dp', 'ctx'), may hold values from -4.5 to 4.5
- cotangent: bfloat16 [4, 32768, 1024], P('dp', 'ctx'), may hold values from -6 to 6
- gain: float32 [1024], replicated, may hold values from 0.1 to 1.9
Outputs:
- attended: bfloat16 [4, 32768, 1024], P('dp', 'ctx')
- grad_queries: bfloat16 [4, 32768, 1024], P('dp', 'ctx')
- grad_keys: bfloat16 [4, 32768, 1024], P('dp', 'ctx')
- grad_values: bfloat16 [4, 32768, 1024], P('dp', 'ctx')
- gain_grad: float32 [1024], replicated
All inputs are finite; a program needn't handle non-finite values.
Results may differ from a plain program's by a relative error of at most 0.019.
The roundings to bfloat16 on the way count: a program that leaves them out, or rounds other values in their place, can miss the bound.
Values may be sent and summed in bfloat16 or wider, within the bound.
A program may use at most 192 MiB of HBM per device.

v0:
```python
import jax
import jax.numpy as jnp
from jax import lax
from jax.sharding import PartitionSpec as P

H = 8
HD = 128
BLOCK = 128
STRIDE = 1024
SUMMARY = 8
NEG = -1e30


def from_behind(value, axis, steps):
    count = lax.axis_size(axis)
    first, last = (max(0, -steps), min(count, count - steps))
    return lax.ppermute(value, axis, [(source, source + steps) for source in range(first, last)])


def to_rows(block_array):
    batch, blocks, heads, width = block_array.shape
    return block_array.transpose(0, 2, 1, 3).reshape(batch, heads, blocks * width)


def to_blocks(row_array, blocks):
    batch, heads, length = row_array.shape
    return row_array.reshape(batch, heads, blocks, length // blocks).transpose(0, 2, 1, 3)


def per_device(queries, keys, values, cotangent, gain):
    f32 = jnp.float32
    bf16 = jnp.bfloat16
    batch, length, width = queries.shape
    blocks = length // BLOCK
    segs = length // STRIDE
    own_sums = segs * SUMMARY
    ctx_count = lax.axis_size("ctx")
    rank = lax.axis_index("ctx")
    scale = HD ** (-0.5)
    scaled = (queries.astype(f32) * gain).astype(bf16)
    rim_keys, rim_values = from_behind(
        (keys[:, length - BLOCK :], values[:, length - BLOCK :]), "ctx", 1
    )
    own_sum_keys = keys.reshape(batch, segs, STRIDE, width)[:, :, STRIDE - SUMMARY :].reshape(
        batch, own_sums, width
    )
    own_sum_values = values.reshape(batch, segs, STRIDE, width)[:, :, STRIDE - SUMMARY :].reshape(
        batch, own_sums, width
    )
    sum_keys, sum_values = (
        lax.all_gather(own_sum_keys, "ctx", axis=1, tiled=True),
        lax.all_gather(own_sum_values, "ctx", axis=1, tiled=True),
    )
    total_sums = sum_keys.shape[1]
    sum_keys = sum_keys.reshape(batch, total_sums, H, HD)
    sum_values = sum_values.reshape(batch, total_sums, H, HD)
    ext_keys = jnp.concatenate([rim_keys, keys], 1).reshape(batch, blocks + 1, BLOCK, H, HD)
    ext_values = jnp.concatenate([rim_values, values], 1).reshape(batch, blocks + 1, BLOCK, H, HD)
    band_keys = jnp.concatenate([ext_keys[:, :-1], ext_keys[:, 1:]], 2)
    band_values = jnp.concatenate([ext_values[:, :-1], ext_values[:, 1:]], 2)
    query_blocks = scaled.reshape(batch, blocks, BLOCK, H, HD)
    scaled_rows = scaled.reshape(batch, length, H, HD)
    grad_rows = cotangent.reshape(batch, length, H, HD)
    grad_blocks = cotangent.reshape(batch, blocks, BLOCK, H, HD)
    query_index = jnp.arange(BLOCK, dtype=jnp.int32)[:, None]
    key_index = jnp.arange(2 * BLOCK, dtype=jnp.int32)[None, :]
    band = (key_index > query_index) & (key_index <= query_index + BLOCK)
    global_block = rank * blocks + jnp.arange(blocks, dtype=jnp.int32)
    band_mask = band[None] & ((global_block > 0)[:, None, None] | (key_index >= BLOCK)[None])
    band_mask = band_mask[None, :, None]
    slot = jnp.arange(total_sums, dtype=jnp.int32)
    sum_pos = slot // SUMMARY * STRIDE + STRIDE - SUMMARY + slot % SUMMARY
    query_pos = rank * length + jnp.arange(length, dtype=jnp.int32)
    sum_mask = (query_pos[:, None] - sum_pos[None, :] >= BLOCK)[None, None]
    band_scores = (
        jnp.einsum("bnqhd,bnkhd->bnhqk", query_blocks, band_keys, preferred_element_type=f32)
        * scale
    )
    band_scores = jnp.where(band_mask, band_scores, NEG)
    sum_scores = (
        jnp.einsum("bqhd,bshd->bhqs", scaled_rows, sum_keys, preferred_element_type=f32) * scale
    )
    sum_scores = jnp.where(sum_mask, sum_scores, NEG)
    top = jnp.maximum(to_rows(jnp.max(band_scores, -1)), jnp.max(sum_scores, -1))
    band_exp = jnp.where(band_mask, jnp.exp(band_scores - to_blocks(top, blocks)[..., None]), 0.0)
    sum_exp = jnp.where(sum_mask, jnp.exp(sum_scores - top[..., None]), 0.0)
    total = to_rows(jnp.sum(band_exp, -1)) + jnp.sum(sum_exp, -1)
    band_prob = band_exp / to_blocks(total, blocks)[..., None]
    sum_prob = sum_exp / total[..., None]
    band_prob_b = band_prob.astype(bf16)
    sum_prob_b = sum_prob.astype(bf16)
    mixed = jnp.einsum(
        "bnhqk,bnkhd->bnqhd", band_prob_b, band_values, preferred_element_type=f32
    ).reshape(batch, length, H, HD)
    mixed = mixed + jnp.einsum(
        "bhqs,bshd->bqhd", sum_prob_b, sum_values, preferred_element_type=f32
    )
    attended = mixed.reshape(batch, length, width).astype(bf16)
    delta = jnp.sum(
        grad_rows.astype(f32) * attended.reshape(batch, length, H, HD).astype(f32), -1
    ).transpose(0, 2, 1)
    band_dprob = jnp.einsum(
        "bnqhd,bnkhd->bnhqk", grad_blocks, band_values, preferred_element_type=f32
    )
    sum_dprob = jnp.einsum("bqhd,bshd->bhqs", grad_rows, sum_values, preferred_element_type=f32)
    band_ds = (band_prob * (band_dprob - to_blocks(delta, blocks)[..., None]) * scale).astype(bf16)
    sum_ds = (sum_prob * (sum_dprob - delta[..., None]) * scale).astype(bf16)
    band_dv = jnp.einsum("bnhqk,bnqhd->bnkhd", band_prob_b, grad_blocks, preferred_element_type=f32)
    band_dk = jnp.einsum("bnhqk,bnqhd->bnkhd", band_ds, query_blocks, preferred_element_type=f32)
    rim_dk, rim_dv = from_behind((band_dk[:, 0, :BLOCK], band_dv[:, 0, :BLOCK]), "ctx", -1)
    sum_dv = jnp.einsum(
        "bhqs,bqhd->bshd", sum_prob_b, grad_rows, preferred_element_type=f32
    ).reshape(batch, total_sums, width)
    sum_dk = jnp.einsum("bhqs,bqhd->bshd", sum_ds, scaled_rows, preferred_element_type=f32).reshape(
        batch, total_sums, width
    )
    whole_dk, whole_dv = lax.psum((sum_dk, sum_dv), "ctx")
    owned_dk = lax.dynamic_slice_in_dim(whole_dk, rank * own_sums, own_sums, 1)
    owned_dv = lax.dynamic_slice_in_dim(whole_dv, rank * own_sums, own_sums, 1)

    def fold_band(pairs, received, owned):
        later = jnp.concatenate([pairs[:, 1:, :BLOCK], received[:, None]], 1)
        folded = (pairs[:, :, BLOCK:] + later).reshape(batch, segs, STRIDE, width)
        folded = folded.at[:, :, STRIDE - SUMMARY :].add(owned.reshape(batch, segs, SUMMARY, width))
        return folded.reshape(batch, length, width).astype(bf16)

    grad_values = fold_band(band_dv, rim_dv, owned_dv)
    grad_keys = fold_band(band_dk, rim_dk, owned_dk)
    grad_scaled = jnp.einsum(
        "bnhqk,bnkhd->bnqhd", band_ds, band_keys, preferred_element_type=f32
    ).reshape(batch, length, H, HD)
    grad_scaled = grad_scaled + jnp.einsum(
        "bhqs,bshd->bqhd", sum_ds, sum_keys, preferred_element_type=f32
    )
    grad_scaled = grad_scaled.reshape(batch, length, width)
    grad_queries = (grad_scaled * gain).astype(bf16)
    gain_part = jnp.sum(grad_scaled * queries.astype(f32), (0, 1))
    gain_total = lax.psum(gain_part, ("dp", "ctx"))
    token_count = batch * lax.axis_size("dp") * length * ctx_count
    gain_grad = gain_total * token_count ** (-0.5)
    return (attended, grad_queries, grad_keys, grad_values, gain_grad)


def solution(mesh):
    in_specs = (
        P("dp", "ctx", None),
        P("dp", "ctx", None),
        P("dp", "ctx", None),
        P("dp", "ctx", None),
        P(),
    )
    out_specs = (
        P("dp", "ctx", None),
        P("dp", "ctx", None),
        P("dp", "ctx", None),
        P("dp", "ctx", None),
        P(),
    )
    return jax.shard_map(
        per_device, mesh=mesh, in_specs=in_specs, out_specs=out_specs, check_vma=False
    )
```

profile of v0, /device:TPU:8, one launch (start us, length us, event | category | flops | bytes accessed | tf_op | source)
XLA Modules:
  0.0 754.5 jit_solution(17129775396608550831)
XLA Ops:
  9.0 4.2 collective-permute-start
  14.9 4.8 collective-permute-start.1
  26.7 93.4 %all-gather = bf16[1,1,256,1024]{3,2,1,0:T(8,128)(2,1)S(1)} all-gather(bf16[1,1,8,1024]{3,2,1,0:T(8,128)(2,1)S(1)} %slice.118), channel_id=2, replica_groups=mesh['dp'=4,'ctx'=32] {'ctx'}, dimensions={2}, use_global_device_ids=true | all-gather | bytes 540672 | tf_op jit(solution)/shard_map/all_gather | solution.py:51
  120.3 95.3 %all-gather.1 = bf16[1,1,256,1024]{3,2,1,0:T(8,128)(2,1)} all-gather(bf16[1,1,8,1024]{3,2,1,0:T(8,128)(2,1)S(1)} %slice.121), channel_id=3, replica_groups=mesh['dp'=4,'ctx'=32] {'ctx'}, dimensions={2}, use_global_device_ids=true | all-gather | bytes 540672 | tf_op jit(solution)/shard_map/all_gather | solution.py:52
  219.8 6.6 fusion.3
  230.4 4.1 copy.86
  251.7 5.2 fusion.2
  256.9 5.7 fusion.5
  274.6 4.3 copy.81
  279.0 5.4 copy.84
  284.4 9.3 %convolution_bitcast_fusion = f32[1,8,256,8,128]{4,2,3,1,0:T(8,128)} fusion(bf16[8,128,8,128]{3,2,1,0:T(8,128)(2,1)} %bitcast.200, f32[8,8,128,256]{3,2,1,0:T(8,128)} %get-tuple-element.53, f32[8,8,128]{2,1,0:T(8,128)S(1)} %fusion.28, f32[8,8,128]{2,1,0:T(8,128)S(1)} %fusion.29, pred[8,128,256]{2,1,0:T(8,128)(4,1)S(1)} %broadcast_and_fusion), kind=kOutput, calls=%fused_computation.27 | convolution fusion | flops 549453824 | bytes 19202048 | tf_op jit(solution)/shard_map/bnhqk,bnqhd->bnkhd/dot_general | solution.py:108
  293.8 6.1 fusion.16
  300.0 7.2 multiply_reduce_fusion
  307.1 17.9 %fusion.1 = bf16[8,8,128,256]{3,2,1,0:T(8,128)(2,1)S(1)} fusion(f32[8,8,128]{2,1,0:T(8,128)} %bitcast.208, bf16[1,8,128,8,128]{4,2,3,1,0:T(8,128)(2,1)} %copy-done.17, bf16[1,8,128,8,128]{4,2,3,1,0:T(8,128)(2,1)} %copy-done.16, bf16[8,128,8,128]{3,2,1,0:T(8,128)(2,1)} %bitcast.201, f32[8,8,128]{2,1,0:T(8,128)} %copy-done.25, f32[8,8,128]{2,1,0:T(8,128)} %copy-done.21, ...), kind=kOutput, calls=%fused_computation.2 | convolution fusion | flops 564133888 | bytes 19234816 | tf_op jit(solution)/shard_map/bnqhd,bnkhd->bnhqk/dot_general | solution.py:102
  325.1 4.4 fusion.14
  329.5 4.4 copy.88
  333.9 5.5 copy.93
  339.4 8.1 %multiply_convert_fusion = bf16[8,1024,256]{1,2,0:T(8,128)(2,1)S(1)} fusion(f32[8,1024]{1,0:T(8,128)S(1)} %bitcast.209, bf16[1024,8,128]{0,2,1:T(8,128)(2,1)} %bitcast.198, bf16[256,8,128]{0,2,1:T(8,128)(2,1)} %bitcast.206, f32[8,1024]{1,0:T(8,128)S(1)} %copy-done.24, f32[8,1024]{1,0:T(8,128)S(1)} %copy-done.20, f32[8,1024,256]{1,2,0:T(8,128)} %get-tuple-element.55, ...), kind=kOutput, calls=%fused_computation.3 | convolution fusion | flops 555745280 | bytes 15564800 | tf_op jit(solution)/shard_map/bqhd,bshd->bhqs/dot_general | solution.py:105
  353.0 5.4 copy.94
  361.7 4.2 convolution_bitcast_fusion.1
  373.4 68.5 %psum.23 = f32[1024]{0:T(1024)S(1)} all-reduce(f32[1024]{0:T(1024)S(1)} %get-tuple-element.46), channel_id=1, replica_groups=mesh['dp'=4,'ctx'=32] {'dp','ctx'}, use_global_device_ids=true, to_apply=%region_8.9 | all-reduce | flops 1024 | bytes 8192 | tf_op jit(solution)/shard_map/psum | solution.py:138
  442.5 4.3 slice.123
  446.8 4.5 slice.127
  453.8 6.3 slice_add_fusion.1
  460.1 5.6 copy.96
  469.8 4.4 copy.103
  474.2 7.2 copy.138
  483.3 238.8 %all-reduce.3.cloned.1.call-done = (f32[1,256,1024]{1,2,0:T(8,128)}, f32[1,256,1024]{1,2,0:T(8,128)}) async-done(((f32[1,256,1024]{1,2,0:T(8,128)}, f32[1,256,1024]{1,2,0:T(8,128)}), (f32[1,256,1024]{1,2,0:T(8,128)}, f32[1,256,1024]{1,2,0:T(8,128)})) %all-reduce.3.cloned.1.call-update) | async-done | bytes 2097168 | tf_op jit(solution)/shard_map/psum | solution.py:117
  725.4 7.1 convert_element_type.88
  732.5 4.5 copy.111
  737.8 5.1 convert_element_type.87
  742.9 4.3 copy.110
  (134 shorter events, 77.4 us)
Async XLA Ops:
  7.2 16.1 %copy-start.22 = (f32[1024]{0:T(1024)S(1)}, f32[1024]{0:T(1024)}, u32[]{:S(2)}) copy-start(f32[1024]{0:T(1024)} %param.13) | copy-start | bytes 12292
  7.2 16.1 %copy-start.2 = (bf16[1,1024,1024]{2,1,0:T(8,128)(2,1)S(1)}, bf16[1,1024,1024]{2,1,0:T(8,128)(2,1)}, u32[]{:S(2)}) copy-start(bf16[1,1024,1024]{2,1,0:T(8,128)(2,1)} %param.9) | copy-start | bytes 6291460
  7.2 714.9 %all-reduce.3.cloned.1.call-start = ((), (), s32[]{:S(2)}) async-start(), calls=%async_computation | async-start | bytes 4194304 | tf_op jit(solution)/shard_map/psum | solution.py:117
  9.0 256.1 %collective-permute-start = (bf16[1,128,1024]{2,1,0:T(8,128)(2,1)}, bf16[1,128,1024]{2,1,0:T(8,128)(2,1)S(1)}, u32[]{:S(2)}, u32[]{:S(2)}) collective-permute-start(bf16[1,128,1024]{2,1,0:T(8,128)(2,1)} %slice.100), channel_id=1, source_target_pairs={{0,1},{1,2},{2,3},{3,4},{4,5},{5,6},{6,7},{7,8},{8,9},{9,10},{10,1... | collective-permute-start | bytes 786440 | tf_op jit(solution)/shard_map/ppermute | solution.py:17
  14.9 231.6 %collective-permute-start.1 = (bf16[1,128,1024]{2,1,0:T(8,128)(2,1)}, bf16[1,128,1024]{2,1,0:T(8,128)(2,1)}, u32[]{:S(2)}, u32[]{:S(2)}) collective-permute-start(bf16[1,128,1024]{2,1,0:T(8,128)(2,1)} %slice.103), channel_id=1, source_target_pairs={{0,1},{1,2},{2,3},{3,4},{4,5},{5,6},{6,7},{7,8},{8,9},{9,10},{10,1... | collective-permute-start | bytes 786440 | tf_op jit(solution)/shard_map/ppermute | solution.py:17
  250.7 6.2 copy-start.10
  250.7 12.0 %slice-start = ((s8[8388608]{0:T(1024)(128)(4,1)}), s8[4194304]{0:T(1024)(128)(4,1)S(1)}, s32[]{:S(2)}) async-start(s8[8388608]{0:T(1024)(128)(4,1)} %bitcast.171), calls=%async_computation.1 | async-start | bytes 8388608
  251.7 5.2 copy-start.12
  251.7 11.0 %slice-start.1 = ((s8[8388608]{0:T(1024)(128)(4,1)}), s8[4194304]{0:T(1024)(128)(4,1)S(1)}, s32[]{:S(2)}) async-start(s8[8388608]{0:T(1024)(128)(4,1)} %bitcast.171), calls=%async_computation.2 | async-start | bytes 8388608
  256.9 43.0 %copy-start.19 = (f32[8,1024]{1,0:T(8,128)}, f32[8,1024]{1,0:T(8,128)S(1)}, u32[]{:S(2)}) copy-start(f32[8,1024]{1,0:T(8,128)S(1)} %bitcast_maximum_fusion) | copy-start | bytes 98308
  256.9 27.5 %copy-start.21 = (f32[8,8,128]{2,1,0:T(8,128)}, f32[8,8,128]{2,1,0:T(8,128)S(1)}, u32[]{:S(2)}) copy-start(f32[8,8,128]{2,1,0:T(8,128)S(1)} %fusion.29) | copy-start | bytes 98308
  265.1 34.9 %copy-start.23 = (f32[8,1024]{1,0:T(8,128)}, f32[8,1024]{1,0:T(8,128)S(1)}, u32[]{:S(2)}) copy-start(f32[8,1024]{1,0:T(8,128)S(1)} %bitcast_add_fusion.2) | copy-start | bytes 98308
  265.1 19.3 %copy-start.25 = (f32[8,8,128]{2,1,0:T(8,128)}, f32[8,8,128]{2,1,0:T(8,128)S(1)}, u32[]{:S(2)}) copy-start(f32[8,8,128]{2,1,0:T(8,128)S(1)} %fusion.28) | copy-start | bytes 98308
  267.4 7.2 copy-start.16
  284.4 9.3 %copy-start.14 = (bf16[1,1024,1024]{1,2,0:T(8,128)(2,1)S(1)}, bf16[1,1024,1024]{1,2,0:T(8,128)(2,1)}, u32[]{:S(2)}) copy-start(bf16[1,1024,1024]{1,2,0:T(8,128)(2,1)} %copy.126) | copy-start | bytes 6291460
  284.4 15.5 %slice-start.2 = ((s8[8388608]{0:T(1024)(128)(4,1)}), s8[4194304]{0:T(1024)(128)(4,1)S(1)}, s32[]{:S(2)}) async-start(s8[8388608]{0:T(1024)(128)(4,1)} %bitcast.173), calls=%async_computation.3 | async-start | bytes 8388608
  293.8 6.2 slice-start.3
  293.8 6.2 copy-start.18
  293.8 13.4 %slice-start.6 = ((s8[8388608]{0:T(1024)(128)(4,1)}), s8[4194304]{0:T(1024)(128)(4,1)S(1)}, s32[]{:S(2)}) async-start(s8[8388608]{0:T(1024)(128)(4,1)} %bitcast.189), calls=%async_computation.7 | async-start | bytes 8388608
  300.0 7.2 slice-start.7
  307.1 17.9 %copy-start.11 = (bf16[1,8,128,8,128]{4,2,3,1,0:T(8,128)(2,1)S(1)}, bf16[1,8,128,8,128]{4,2,3,1,0:T(8,128)(2,1)}, u32[]{:S(2)}) copy-start(bf16[1,8,128,8,128]{4,2,3,1,0:T(8,128)(2,1)} %copy-done.10) | copy-start | bytes 6291460
  325.1 4.4 copy-start.1
  333.9 5.5 copy-start.20
  333.9 5.5 copy-start.24
  333.9 5.5 copy-start.26
  339.4 8.1 %copy-start.3 = (bf16[1,1024,1024]{1,2,0:T(8,128)(2,1)S(1)}, bf16[1,1024,1024]{1,2,0:T(8,128)(2,1)}, u32[]{:S(2)}) copy-start(bf16[1,1024,1024]{1,2,0:T(8,128)(2,1)} %copy.125) | copy-start | bytes 6291460
  360.4 105.3 %collective-permute-start.3 = (f32[1,128,8,128]{3,1,2,0:T(8,128)}, f32[1,128,8,128]{3,1,2,0:T(8,128)S(1)}, u32[]{:S(2)}, u32[]{:S(2)}) collective-permute-start(f32[1,128,8,128]{3,1,2,0:T(8,128)} %slice_bitcast_fusion), channel_id=1, source_target_pairs={{1,0},{2,1},{3,2},{4,3},{5,4},{6,5},{7,6},{8,7},{9,8},{10,9},{11,1... | collective-permute-start | bytes 1572872 | tf_op jit(solution)/shard_map/ppermute | solution.py:17
  361.7 9.6 %copy-start.6 = (f32[1,1024,1024]{2,1,0:T(8,128)S(1)}, f32[1,1024,1024]{2,1,0:T(8,128)}, u32[]{:S(2)}) copy-start(f32[1,1024,1024]{2,1,0:T(8,128)} %copy.94) | copy-start | bytes 12582916
  370.0 83.8 %collective-permute-start.2 = (f32[1,128,8,128]{1,3,2,0:T(8,128)}, f32[1,128,8,128]{1,3,2,0:T(8,128)S(1)}, u32[]{:S(2)}, u32[]{:S(2)}) collective-permute-start(f32[1,128,8,128]{1,3,2,0:T(8,128)} %slice_bitcast_fusion.1), channel_id=1, source_target_pairs={{1,0},{2,1},{3,2},{4,3},{5,4},{6,5},{7,6},{8,7},{9,8},{10,9},{11,1... | collective-permute-start | bytes 1572872 | tf_op jit(solution)/shard_map/ppermute | solution.py:17
  446.8 4.5 copy-start.15
  474.2 7.2 copy-start.4
  732.5 4.5 copy-start.7
  (8 other events, 23.9 us)
Sparse Core Ops, SparseCore 0:
  361.8 360.2 all-reduce.2
where the time goes:
time: 765 us; the launch traced here: 754 us
  blocking collectives  257 us (34%)
  waiting for transfers between devices  239 us (31%)
  local copies, waits for them, and re-layouts  109 us (14%)
  matrix products  78.5 us (10%)
  other arithmetic  44.2 us (6%)
  between operations  15 us (2%)
  starting transfers between devices  11.6 us (2%)
    psum x1, waiting for transfers between devices, per_device(): whole_dk, whole_dv = lax.psum((sum_dk, sum_dv), 'ctx')  239 us
    all_gather x1, blocking collectives, per_device(): lax.all_gather(own_sum_values, 'ctx', axis=1, tiled=True)  95.3 us
    all_gather x1, blocking collectives, per_device(): lax.all_gather(own_sum_keys, 'ctx', axis=1, tiled=True)  93.4 us
    psum x1, blocking collectives, per_device(): gain_total = lax.psum(gain_part, ('dp', 'ctx'))  68.5 us
    unnamed x83, local copies, waits for them, and re-layouts  36.2 us
    dot_general x1, matrix products, per_device(): jnp.einsum('bnqhd,bnkhd->bnhqk', grad_blocks, band_values, preferred_elem...  17.9 us
  transfers between devices with their start and end apart: 5, of which 1 were waited for; matrix products, arithmetic and copies ran while one was open for 14% of the time, Pallas kernels for 0%

commit v1 on v0

--- a/solution.py
+++ b/solution.py
@@ -48,7 +48,9 @@
         batch, own_sums, width
     )
     sum_keys, sum_values = (
-        lax.all_gather(own_sum_keys, "ctx", axis=1, tiled=True),
+        jnp.concatenate(
+            lax.all_to_all(jnp.stack([own_sum_keys] * lax.axis_size("ctx")), "ctx", 0, 0), axis=1
+        ),
         lax.all_gather(own_sum_values, "ctx", axis=1, tiled=True),
     )
     total_sums = sum_keys.shape[1]

time: 765 us -> 682 us (0.89)
  blocking collectives: 257 us -> 171 us
  starting transfers between devices: 11.6 us -> 20.5 us
    all_gather x1 -> x0, blocking collectives: 93.4 us -> none  [per_device(): lax.all_gather(own_sum_keys, 'ctx', axis=1, tiled=True)]
    all_to_all x0 -> x1, starting transfers between devices: none -> 8.89 us  [per_device(): lax.all_to_all(jnp.stack([own_sum_keys] * lax.axis_size('ctx')), 'ctx', 0...]
    unnamed x83 -> x82, local copies, waits for them, and re-layouts: 36.2 us -> 37.5 us
  transfers between devices with their start and end apart: 5 -> 6, of which waited for: 1 -> 1; matrix products, arithmetic and copies ran while one was open for 14% -> 15% of each run, Pallas kernels for 0% -> 0%
where the time goes in v1:
time: 682 us; the launch traced here: 671 us
  waiting for transfers between devices  235 us (34%)
  blocking collectives  171 us (25%)
  local copies, waits for them, and re-layouts  113 us (17%)
  matrix products  75 us (11%)
  other arithmetic  41.7 us (6%)
  starting transfers between devices  20.5 us (3%)
  between operations  15.1 us (2%)
    psum x1, waiting for transfers between devices, per_device(): whole_dk, whole_dv = lax.psum((sum_dk, sum_dv), 'ctx')  235 us
    all_gather x1, blocking collectives, per_device(): lax.all_gather(own_sum_values, 'ctx', axis=1, tiled=True)  102 us
    psum x1, blocking collectives, per_device(): gain_total = lax.psum(gain_part, ('dp', 'ctx'))  68.7 us
    unnamed x82, local copies, waits for them, and re-layouts  37.5 us
    dot_general x1, matrix products, per_device(): jnp.einsum('bnqhd,bnkhd->bnhqk', grad_blocks, band_values, preferred_elem...  17.4 us
  transfers between devices with their start and end apart: 6, of which 1 were waited for; matrix products, arithmetic and copies ran while one was open for 15% of the time, Pallas kernels for 0%

profile of v1, /device:TPU:8, one launch (start us, length us, event | category | flops | bytes accessed | tf_op | source)
XLA Modules:
  0.0 671.3 jit_solution(14463277451742916610)
XLA Ops:
  9.0 4.2 collective-permute-start
  14.9 4.8 collective-permute-start.1
  21.3 8.9 %all-to-all-start = ((bf16[32,1,8,1024]{3,2,1,0:T(8,128)(2,1)}), bf16[32,1,8,1024]{3,2,1,0:T(8,128)(2,1)S(1)}, u32[]{:S(2)}, u32[]{:S(2)}) async-start(bf16[32,1,8,1024]{3,2,1,0:T(8,128)(2,1)} %stack.3), calls=%async_computation | async-start | bytes 1048576 | tf_op jit(solution)/shard_map/all_to_all | solution.py:52
  36.5 102.5 %all-gather = bf16[1,1,256,1024]{3,2,1,0:T(8,128)(2,1)} all-gather(bf16[1,1,8,1024]{3,2,1,0:T(8,128)(2,1)S(1)} %slice.124), channel_id=2, replica_groups=mesh['dp'=4,'ctx'=32] {'ctx'}, dimensions={2}, use_global_device_ids=true | all-gather | bytes 540672 | tf_op jit(solution)/shard_map/all_gather | solution.py:54
  143.3 4.1 copy.85
  155.2 4.1 copy.95
  174.3 5.1 fusion.2
  195.4 4.3 copy.80
  199.7 5.4 copy.83
  205.2 9.3 %convolution_bitcast_fusion = f32[1,8,256,8,128]{4,2,3,1,0:T(8,128)} fusion(bf16[8,128,8,128]{3,2,1,0:T(8,128)(2,1)} %bitcast.199, f32[8,8,128,256]{3,2,1,0:T(8,128)} %get-tuple-element.53, f32[8,8,128]{2,1,0:T(8,128)S(1)} %fusion.28, f32[8,8,128]{2,1,0:T(8,128)S(1)} %fusion.29, pred[8,128,256]{2,1,0:T(8,128)(4,1)S(1)} %broadcast_and_fusion), kind=kOutput, calls=%fused_computation.27 | convolution fusion | flops 549453824 | bytes 19202048 | tf_op jit(solution)/shard_map/bnhqk,bnqhd->bnkhd/dot_general | solution.py:110
  214.5 6.2 fusion.16
  220.7 7.3 %multiply_reduce_fusion = (f32[1024,8]{0,1:T(8,128)}, bf16[1,1024,8,128]{1,3,2,0:T(8,128)(2,1)}) fusion(f32[1,1024,8,128]{1,3,2,0:T(8,128)} %bitcast.194, f32[1,1024,8,128]{1,3,2,0:T(8,128)} %copy.83, bf16[256,8,128]{0,2,1:T(8,128)(2,1)S(1)} %bitcast.208, f32[8,1024]{1,0:T(8,128)S(1)} %bitcast_add_fusion.2, f32[8,1024]{1,0:T(8,128)S(1)} %bitcast_maximum_fusion, ...), kind=kOutput, calls=%fused_computation.26 | convolution fusion | flops 554688512 | bytes 19759104 | tf_op jit(solution)/shard_map/bhqs,bshd->bqhd/dot_general | solution.py:97
  228.0 17.4 %fusion.1 = bf16[8,8,128,256]{3,2,1,0:T(8,128)(2,1)S(1)} fusion(f32[8,8,128]{2,1,0:T(8,128)} %bitcast.209, bf16[1,8,128,8,128]{4,2,3,1,0:T(8,128)(2,1)} %copy.123, bf16[1,8,128,8,128]{4,2,3,1,0:T(8,128)(2,1)} %copy.122, bf16[8,128,8,128]{3,2,1,0:T(8,128)(2,1)} %bitcast.200, f32[8,8,128]{2,1,0:T(8,128)} %copy-done.28, f32[8,8,128]{2,1,0:T(8,128)} %copy-done.23, ...), kind=kOutput, calls=%fused_computation.2 | convolution fusion | flops 564133888 | bytes 19234816 | tf_op jit(solution)/shard_map/bnqhd,bnkhd->bnhqk/dot_general | solution.py:104
  245.4 4.4 fusion.14
  249.9 4.4 copy.87
  254.3 5.4 copy.93
  259.7 8.1 %multiply_convert_fusion = bf16[8,1024,256]{1,2,0:T(8,128)(2,1)S(1)} fusion(f32[8,1024]{1,0:T(8,128)S(1)} %bitcast.210, bf16[1024,8,128]{0,2,1:T(8,128)(2,1)} %bitcast.197, bf16[256,8,128]{0,2,1:T(8,128)(2,1)} %bitcast.207, f32[8,1024]{1,0:T(8,128)S(1)} %copy-done.27, f32[8,1024]{1,0:T(8,128)S(1)} %copy-done.22, f32[8,1024,256]{1,2,0:T(8,128)} %copy-done.1, ...), kind=kOutput, calls=%fused_computation.3 | convolution fusion | flops 555745280 | bytes 15564800 | tf_op jit(solution)/shard_map/bqhd,bshd->bhqs/dot_general | solution.py:107
  273.3 5.4 copy.94
  282.0 4.2 convolution_bitcast_fusion.1
  293.7 68.7 %psum.23 = f32[1024]{0:T(1024)S(1)} all-reduce(f32[1024]{0:T(1024)S(1)} %get-tuple-element.46), channel_id=1, replica_groups=mesh['dp'=4,'ctx'=32] {'dp','ctx'}, use_global_device_ids=true, to_apply=%region_8.9 | all-reduce | flops 1024 | bytes 8192 | tf_op jit(solution)/shard_map/psum | solution.py:140
  362.9 4.3 slice.126
  367.3 4.4 slice.130
  374.2 6.3 slice_add_fusion.1
  380.6 5.6 copy.96
  386.2 4.1 slice_add_fusion
  390.3 4.4 copy.103
  394.7 7.2 %copy.138 = f32[1,1024,1024]{2,0,1:T(1,128)} copy(f32[1,1024,1024]{2,0,1:T(1,128)} %bitcast.185) | data formatting | bytes 8388608
  403.8 235.2 %all-reduce.3.cloned.1.call-done = (f32[1,256,1024]{1,2,0:T(8,128)}, f32[1,256,1024]{1,2,0:T(8,128)}) async-done(((f32[1,256,1024]{1,2,0:T(8,128)}, f32[1,256,1024]{1,2,0:T(8,128)}), (f32[1,256,1024]{1,2,0:T(8,128)}, f32[1,256,1024]{1,2,0:T(8,128)})) %all-reduce.3.cloned.1.call-update) | async-done | bytes 2097168 | tf_op jit(solution)/shard_map/psum | solution.py:119
  642.3 7.1 %convert_element_type.88 = bf16[1,1024,1024]{2,0,1:T(2,128)(2,1)} convert(f32[1,1024,1024]{2,0,1:T(1,128)} %fusion.25) | non-fusion elementwise | flops 1048576 | bytes 6291456 | tf_op jit(solution)/shard_map/convert_element_type | solution.py:127
  649.3 4.5 copy.111
  654.6 5.1 convert_element_type.87
  659.7 4.3 copy.110
  (133 shorter events, 79.5 us)
Async XLA Ops:
  7.2 26.6 %copy-start.25 = (f32[1024]{0:T(1024)S(1)}, f32[1024]{0:T(1024)}, u32[]{:S(2)}) copy-start(f32[1024]{0:T(1024)} %param.13) | copy-start | bytes 12292
  7.2 26.6 %copy-start.3 = (bf16[1,1024,1024]{2,1,0:T(8,128)(2,1)S(1)}, bf16[1,1024,1024]{2,1,0:T(8,128)(2,1)}, u32[]{:S(2)}) copy-start(bf16[1,1024,1024]{2,1,0:T(8,128)(2,1)} %param.9) | copy-start | bytes 6291460
  9.0 159.1 %collective-permute-start = (bf16[1,128,1024]{2,1,0:T(8,128)(2,1)}, bf16[1,128,1024]{2,1,0:T(8,128)(2,1)S(1)}, u32[]{:S(2)}, u32[]{:S(2)}) collective-permute-start(bf16[1,128,1024]{2,1,0:T(8,128)(2,1)} %slice.102), channel_id=1, source_target_pairs={{0,1},{1,2},{2,3},{3,4},{4,5},{5,6},{6,7},{7,8},{8,9},{9,10},{10,1... | collective-permute-start | bytes 786440 | tf_op jit(solution)/shard_map/ppermute | solution.py:17
  14.9 148.4 %collective-permute-start.1 = (bf16[1,128,1024]{2,1,0:T(8,128)(2,1)}, bf16[1,128,1024]{2,1,0:T(8,128)(2,1)}, u32[]{:S(2)}, u32[]{:S(2)}) collective-permute-start(bf16[1,128,1024]{2,1,0:T(8,128)(2,1)} %slice.105), channel_id=1, source_target_pairs={{0,1},{1,2},{2,3},{3,4},{4,5},{5,6},{6,7},{7,8},{8,9},{9,10},{10,1... | collective-permute-start | bytes 786440 | tf_op jit(solution)/shard_map/ppermute | solution.py:17
  21.3 158.2 %all-to-all-start = ((bf16[32,1,8,1024]{3,2,1,0:T(8,128)(2,1)}), bf16[32,1,8,1024]{3,2,1,0:T(8,128)(2,1)S(1)}, u32[]{:S(2)}, u32[]{:S(2)}) async-start(bf16[32,1,8,1024]{3,2,1,0:T(8,128)(2,1)} %stack.3), calls=%async_computation | async-start | bytes 1048576 | tf_op jit(solution)/shard_map/all_to_all | solution.py:52
  30.2 608.8 %all-reduce.3.cloned.1.call-start = ((), (), s32[]{:S(2)}) async-start(), calls=%async_computation.1 | async-start | bytes 4194304 | tf_op jit(solution)/shard_map/psum | solution.py:119
  167.5 6.8 %copy-start.12 = (bf16[1,8,128,8,128]{4,2,3,1,0:T(8,128)(2,1)}, bf16[1,8,128,8,128]{4,2,3,1,0:T(8,128)(2,1)S(1)}, u32[]{:S(2)}) copy-start(bf16[1,8,128,8,128]{4,2,3,1,0:T(8,128)(2,1)S(1)} %copy.120) | copy-start | bytes 6291460
  168.1 6.2 copy-start.14
  170.5 3.8 copy-start.9
  181.7 4.0 copy-start.11
  185.2 35.4 %copy-start.21 = (f32[8,1024]{1,0:T(8,128)}, f32[8,1024]{1,0:T(8,128)S(1)}, u32[]{:S(2)}) copy-start(f32[8,1024]{1,0:T(8,128)S(1)} %bitcast_maximum_fusion) | copy-start | bytes 98308
  185.3 19.9 %copy-start.23 = (f32[8,8,128]{2,1,0:T(8,128)}, f32[8,8,128]{2,1,0:T(8,128)S(1)}, u32[]{:S(2)}) copy-start(f32[8,8,128]{2,1,0:T(8,128)S(1)} %fusion.29) | copy-start | bytes 98308
  191.3 29.4 %copy-start.26 = (f32[8,1024]{1,0:T(8,128)}, f32[8,1024]{1,0:T(8,128)S(1)}, u32[]{:S(2)}) copy-start(f32[8,1024]{1,0:T(8,128)S(1)} %bitcast_add_fusion.2) | copy-start | bytes 98308
  191.3 13.8 %copy-start.28 = (f32[8,8,128]{2,1,0:T(8,128)}, f32[8,8,128]{2,1,0:T(8,128)S(1)}, u32[]{:S(2)}) copy-start(f32[8,8,128]{2,1,0:T(8,128)S(1)} %fusion.28) | copy-start | bytes 98308
  205.1 9.3 %copy-start.16 = (bf16[1,1024,1024]{1,2,0:T(8,128)(2,1)S(1)}, bf16[1,1024,1024]{1,2,0:T(8,128)(2,1)}, u32[]{:S(2)}) copy-start(bf16[1,1024,1024]{1,2,0:T(8,128)(2,1)} %copy.125) | copy-start | bytes 6291460
  205.1 15.5 %slice-start = ((s8[8388608]{0:T(1024)(128)(4,1)}), s8[4194304]{0:T(1024)(128)(4,1)S(1)}, s32[]{:S(2)}) async-start(s8[8388608]{0:T(1024)(128)(4,1)} %bitcast.176), calls=%async_computation.2 | async-start | bytes 8388608
  214.5 6.2 slice-start.1
  214.5 6.2 copy-start.20
  214.5 13.5 %slice-start.2 = ((s8[8388608]{0:T(1024)(128)(4,1)}), s8[4194304]{0:T(1024)(128)(4,1)S(1)}, s32[]{:S(2)}) async-start(s8[8388608]{0:T(1024)(128)(4,1)} %bitcast.190), calls=%async_computation.4 | async-start | bytes 8388608
  220.7 7.3 %slice-start.3 = ((s8[8388608]{0:T(1024)(128)(4,1)}), s8[4194304]{0:T(1024)(128)(4,1)S(1)}, s32[]{:S(2)}) async-start(s8[8388608]{0:T(1024)(128)(4,1)} %bitcast.190), calls=%async_computation.5 | async-start | bytes 8388608
  228.0 17.4 %copy-start.13 = (bf16[1,8,128,8,128]{4,2,3,1,0:T(8,128)(2,1)S(1)}, bf16[1,8,128,8,128]{4,2,3,1,0:T(8,128)(2,1)}, u32[]{:S(2)}) copy-start(bf16[1,8,128,8,128]{4,2,3,1,0:T(8,128)(2,1)} %copy-done.12) | copy-start | bytes 6291460
  245.4 4.4 copy-start.2
  254.3 5.4 copy-start.22
  254.3 5.4 copy-start.27
  254.3 5.4 copy-start.29
  259.7 8.1 %copy-start.4 = (bf16[1,1024,1024]{1,2,0:T(8,128)(2,1)S(1)}, bf16[1,1024,1024]{1,2,0:T(8,128)(2,1)}, u32[]{:S(2)}) copy-start(bf16[1,1024,1024]{1,2,0:T(8,128)(2,1)} %copy.124) | copy-start | bytes 6291460
  280.6 105.5 %collective-permute-start.3 = (f32[1,128,8,128]{3,1,2,0:T(8,128)}, f32[1,128,8,128]{3,1,2,0:T(8,128)S(1)}, u32[]{:S(2)}, u32[]{:S(2)}) collective-permute-start(f32[1,128,8,128]{3,1,2,0:T(8,128)} %slice_bitcast_fusion), channel_id=1, source_target_pairs={{1,0},{2,1},{3,2},{4,3},{5,4},{6,5},{7,6},{8,7},{9,8},{10,9},{11,1... | collective-permute-start | bytes 1572872 | tf_op jit(solution)/shard_map/ppermute | solution.py:17
  281.9 9.6 %copy-start.7 = (f32[1,1024,1024]{2,1,0:T(8,128)S(1)}, f32[1,1024,1024]{2,1,0:T(8,128)}, u32[]{:S(2)}) copy-start(f32[1,1024,1024]{2,1,0:T(8,128)} %copy.94) | copy-start | bytes 12582916
  290.2 84.0 %collective-permute-start.2 = (f32[1,128,8,128]{1,3,2,0:T(8,128)}, f32[1,128,8,128]{1,3,2,0:T(8,128)S(1)}, u32[]{:S(2)}, u32[]{:S(2)}) collective-permute-start(f32[1,128,8,128]{1,3,2,0:T(8,128)} %slice_bitcast_fusion.1), channel_id=1, source_target_pairs={{1,0},{2,1},{3,2},{4,3},{5,4},{6,5},{7,6},{8,7},{9,8},{10,9},{11,1... | collective-permute-start | bytes 1572872 | tf_op jit(solution)/shard_map/ppermute | solution.py:17
  367.3 4.4 copy-start.17
  394.7 7.2 %copy-start.5 = (f32[1,8,128,8,128]{4,3,0,2,1:T(8,128)S(1)}, f32[1,8,128,8,128]{4,3,0,2,1:T(8,128)}, u32[]{:S(2)}) copy-start(f32[1,8,128,8,128]{4,3,0,2,1:T(8,128)} %copy.96) | copy-start | bytes 12582916
  649.3 4.5 copy-start.8
  (8 other events, 23.1 us)
Sparse Core Ops, SparseCore 0:
  282.1 356.8 all-reduce.2
